TPU v7x, 32 devices: a whole 2x2x4 slice. The times are simulated.
32 devices in a mesh: loc: 16 (over z, x, core), yr: 2 (over y).
Axes of the slice: x: 2, y: 2, z: 4, core: 2. Of those that a mesh axis runs over, the one named last changes fastest.
Arguments:
- noise: bfloat16 [2, 111, 512, 1024], P(None, None, ('yr', 'loc')), parts along dimension 2, may hold values from -6 to 6
- loc_factor: bfloat16 [1024, 1024], P('loc'), as said below
- age_factor: bfloat16 [111, 111], replicated, as said below
- mean_rate: float32 [4, 111, 1024], P('yr'), parts along dimension 0, may hold values from -7 to -2
- population: float32 [4, 111, 1024], P('yr'), parts along dimension 0, may hold values from 0.1 to 10
- region_of: int32 [1024, 1], replicated, may hold values from 0 to 63
Outputs:
- log_rates: bfloat16 [2, 111, 1024, 512], P(None, None, 'loc', 'yr'), parts along dimension 3
- loc_survival: float32 [2, 1024, 512], P(None, 'loc', 'yr'), parts along dimension 2
- region_survival: float32 [2, 64, 512], P(None, 'loc', 'yr'), parts along dimension 2
There are 2 independent parts, one for each index of `yr`. A program takes and returns all parts, laid end to end along the dimension named above; an argument that names none is the same for every part. Nothing has to cross between parts.
Inputs may be any that keep to these rules, and one draw needn't show every extreme that they name: `region_of`: every region holds at least one location. `loc_factor`: lower triangular with a positive diagonal. `age_factor`: lower triangular with a positive diagonal.
All inputs are finite; a program needn't handle non-finite values.
Results may differ from a plain program's by a relative error of at most 0.006.
Values may be sent and summed in bfloat16 or wider, within the bound.
No kernel may reach another device: no remote copies, remote signals or barrier semaphores. Data moves between devices by JAX's collectives and lax.ppermute only.
A program may use at most 128 MiB of HBM per device.

v0:
```python
import jax
import jax.numpy as jnp
from jax import lax
from jax.sharding import PartitionSpec as P

REGIONS = 64


def survival(rates):
    hazard = jnp.cumsum(rates, axis=1)
    after = jnp.exp(-hazard)
    total = 0.5 + jnp.sum(after, axis=1) - 0.5 * after[:, -1]
    return total / rates.shape[1]


def shards(noise, loc_factor, age_factor, mean_rate, population, region_of):
    highest = lax.Precision.HIGHEST
    regions_all = REGIONS
    spread = jnp.einsum(
        "sark,lk->sarl",
        noise,
        lax.all_gather(loc_factor, "loc", axis=0, tiled=True),
        preferred_element_type=jnp.float32,
    ).astype(jnp.bfloat16)
    mixed = jnp.einsum("ab,sbrl->sarl", age_factor, spread, preferred_element_type=jnp.float32)
    log_section = (mean_rate[:, :, None, :] + mixed).astype(jnp.bfloat16)
    rates = jnp.exp(log_section.astype(jnp.float32))
    onehot = (region_of == jnp.arange(regions_all, dtype=jnp.int32)[None, :]).astype(jnp.float32)
    totals = jnp.einsum("sal,lg->sag", population, onehot, precision=highest)
    weighted = jnp.einsum(
        "sarl,lg->sarg", population[:, :, None, :] * rates, onehot, precision=highest
    )
    region_section = survival(weighted / totals[:, :, None, :])
    region_moved = lax.all_to_all(region_section, "loc", split_axis=2, concat_axis=1, tiled=True)
    region_survival = jnp.transpose(region_moved, (0, 2, 1))
    turned = jnp.transpose(
        lax.all_to_all(log_section, "loc", split_axis=3, concat_axis=2, tiled=True), (0, 1, 3, 2)
    )
    loc_survival = survival(jnp.exp(turned.astype(jnp.float32)))
    return (turned, loc_survival, region_survival)


def solution(mesh):
    placed = (
        P(None, None, ("yr", "loc"), None),
        P("loc", None),
        P(),
        P("yr", None, None),
        P("yr", None, None),
        P(),
    )
    return jax.shard_map(
        shards,
        mesh=mesh,
        in_specs=placed,
        out_specs=(P(None, None, "loc", "yr"), P(None, "loc", "yr"), P(None, "loc", "yr")),
        check_vma=False,
    )
```

profile of v0, /device:TPU:11, one launch (start us, length us, event | category | flops | bytes accessed | tf_op | source)
XLA Modules:
  0.0 370.4 jit_solution(1363313943726732951)
XLA Ops:
  7.2 0.0 copy-start
  7.2 0.0 all-gather.2.cloned.1.call-start
  7.2 0.7 all-gather.2.cloned.1.call-update
  7.9 1.5 copy.50
  9.4 1.5 copy.56
  10.9 2.0 convolution_bitcast_fusion
  12.9 0.0 copy-start.2
  12.9 38.4 %all-gather.2.cloned.1.call-done = bf16[1024,1024]{1,0:T(8,128)(2,1)} async-done(((bf16[64,1024]{1,0:T(8,128)(2,1)}), bf16[1024,1024]{1,0:T(8,128)(2,1)}) %all-gather.2.cloned.1.call-update) | async-done | bytes 2097168 | tf_op jit(solution)/shard_map/all_gather | solution.py:22
  51.3 0.0 copy-done
  51.3 21.3 %fusion = bf16[2,111,16,1024]{3,1,2,0:T(8,128)(2,1)} fusion(f32[2,111,1024]{2,1,0:T(8,128)S(1)} %copy.50, bf16[2,111,16,1024]{3,2,1,0:T(8,128)(2,1)} %param.6, bf16[1024,1024]{1,0:T(8,128)(2,1)} %all-gather.2.cloned.1.call-done, bf16[111,111]{1,0:T(8,128)(2,1)S(1)} %copy-done), kind=kOutput, calls=%fused_computation.1 | convolution fusion | flops 8267464704 | bytes 17580098 | tf_op jit(solution)/shard_map/ab,sbrl->sarl/dot_general | solution.py:25
  72.6 0.0 copy-done.2
  72.6 12.1 %fusion.25 = f32[2,111,16,64]{1,3,2,0:T(8,128)S(1)} fusion(bf16[2,111,16,1024]{3,1,2,0:T(8,128)(2,1)} %fusion, f32[2,111,1024]{2,1,0:T(8,128)S(1)} %copy.56, f32[2,111,64]{1,2,0:T(8,128)S(1)} %convolution_bitcast_fusion, s32[1024]{0:T(1024)S(1)} %bitcast.62), kind=kOutput, calls=%fused_computation.18 | convolution fusion | flops 2800973824 | bytes 9154048 | tf_op jit(solution)/shard_map/sarl,lg->sarg/dot_general | solution.py:30
  84.7 0.9 copy.58
  85.6 36.4 %fusion.44 = f32[2,111,16,64]{3,2,1,0:T(8,128)S(1)} fusion(f32[2,111,16,64]{3,2,1,0:T(8,128)S(1)} %copy.58), kind=kOutput, calls=%fused_computation.36 | output fusion | flops 25006080 | bytes 1818624 | tf_op jit(solution)/shard_map/jit(cumsum)/reduce_window_sum | solution.py:10
  121.9 0.2 fusion.42
  122.2 0.1 copy.59
  122.3 0.7 reshape.17
  123.0 5.7 %all-to-all-start.1 = ((f32[16,1,128]{2,1,0:T(1,128)}), f32[16,1,128]{2,1,0:T(1,128)S(1)}, u32[]{:S(2)}, u32[]{:S(2)}) async-start(f32[16,1,128]{2,1,0:T(1,128)} %reshape.17), calls=%async_computation.1 | async-start | bytes 16384 | tf_op jit(solution)/shard_map/all_to_all | solution.py:34
  128.7 12.3 %copy.52 = bf16[2,111,16,1024]{1,2,0,3:T(8,128)(2,1)} copy(bf16[2,111,16,1024]{3,1,2,0:T(8,128)(2,1)} %fusion) | data formatting | bytes 14548992 | tf_op jit(solution)/shard_map/convert_element_type | solution.py:26
  141.1 0.0 all-to-all-done.1
  141.1 6.0 %all-to-all-start = ((bf16[2,111,16,1024]{1,2,0,3:T(8,128)(2,1)}), bf16[2,111,16,1024]{1,2,0,3:T(8,128)(2,1)}, u32[]{:S(2)}, u32[]{:S(2)}) async-start(bf16[2,111,16,1024]{1,2,0,3:T(8,128)(2,1)} %copy.52), calls=%async_computation | async-start | bytes 16777216 | tf_op jit(solution)/shard_map/all_to_all | solution.py:37
  147.1 0.5 broadcast.27
  147.6 0.7 reduce
  148.3 0.1 reshape.18
  148.4 0.7 all_to_all.33
  149.1 180.3 %all-to-all-done = bf16[2,111,16,1024]{1,2,0,3:T(8,128)(2,1)} async-done(((bf16[2,111,16,1024]{1,2,0,3:T(8,128)(2,1)}), bf16[2,111,16,1024]{1,2,0,3:T(8,128)(2,1)}, u32[]{:S(2)}, u32[]{:S(2)}) %all-to-all-start) | async-done | bytes 7274528 | tf_op jit(solution)/shard_map/all_to_all | solution.py:37
  329.4 9.8 %copy.54 = bf16[2,111,16,16,64]{1,4,3,2,0:T(8,128)(2,1)} copy(bf16[2,111,16,16,64]{1,3,0,4,2:T(8,128)(2,1)} %bitcast.7) | data formatting | bytes 14548992 | tf_op jit(solution)/shard_map/all_to_all | solution.py:37
  339.3 13.5 %copy.55 = bf16[2,111,256,64]{2,3,1,0:T(8,128)(2,1)} copy(bf16[2,111,256,64]{1,3,2,0:T(8,128)(2,1)} %bitcast.54) | data formatting | bytes 14548992 | tf_op jit(solution)/shard_map/all_to_all | solution.py:37
  352.8 0.0 copy-start.1
  352.8 9.1 %fusion.43 = (f32[2,64,256]{2,1,0:T(8,128)S(1)}, f32[2,111,64,256]{3,2,1,0:T(8,128)}) fusion(bf16[2,111,64,256]{3,2,1,0:T(8,128)(2,1)} %bitcast.55), kind=kOutput, calls=%fused_computation.35 | output fusion | flops 410976256 | bytes 21954560 | tf_op jit(solution)/shard_map/jit(cumsum)/reduce_window_sum | solution.py:10
  361.9 1.6 fusion.34
  363.5 0.0 copy-done.1
  (3 shorter events, 0.0 us)
Async XLA Ops:
  7.2 44.1 %copy-start = (bf16[111,111]{1,0:T(8,128)(2,1)S(1)}, bf16[111,111]{1,0:T(8,128)(2,1)}, u32[]{:S(2)}) copy-start(bf16[111,111]{1,0:T(8,128)(2,1)} %param.8) | copy-start | bytes 73930
  7.2 44.1 %all-gather.2.cloned.1.call-start = ((), (), s32[]{:S(2)}) async-start(), calls=%async_computation.2 | async-start | bytes 2228224 | tf_op jit(solution)/shard_map/all_gather | solution.py:22
  12.9 59.7 %copy-start.2 = (s32[1024,1]{0,1:T(1,128)S(1)}, s32[1024,1]{0,1:T(1,128)}, u32[]{:S(2)}) copy-start(s32[1024,1]{0,1:T(1,128)} %param.11) | copy-start | bytes 12292
  123.0 18.0 %all-to-all-start.1 = ((f32[16,1,128]{2,1,0:T(1,128)}), f32[16,1,128]{2,1,0:T(1,128)S(1)}, u32[]{:S(2)}, u32[]{:S(2)}) async-start(f32[16,1,128]{2,1,0:T(1,128)} %reshape.17), calls=%async_computation.1 | async-start | bytes 16384 | tf_op jit(solution)/shard_map/all_to_all | solution.py:34
  141.1 188.4 %all-to-all-start = ((bf16[2,111,16,1024]{1,2,0,3:T(8,128)(2,1)}), bf16[2,111,16,1024]{1,2,0,3:T(8,128)(2,1)}, u32[]{:S(2)}, u32[]{:S(2)}) async-start(bf16[2,111,16,1024]{1,2,0,3:T(8,128)(2,1)} %copy.52), calls=%async_computation | async-start | bytes 16777216 | tf_op jit(solution)/shard_map/all_to_all | solution.py:37
  352.8 10.7 %copy-start.1 = (bf16[111,111]{1,0:T(8,128)(2,1)S(1)}, bf16[111,111]{1,0:T(8,128)(2,1)}, u32[]{:S(2)}) copy-start(bf16[111,111]{1,0:T(8,128)(2,1)} %param.8) | copy-start | bytes 73930
Sparse Core Ops, SparseCore 0:
  10.2 41.0 all-gather.1
where the time goes:
time: 371 us; the launch traced here: 370 us
  waiting for transfers between devices  219 us (59%)
  other arithmetic  48 us (13%)
  local copies, waits for them, and re-layouts  41.7 us (11%)
  matrix products  35.4 us (10%)
  between operations  14.1 us (4%)
  starting transfers between devices  11.7 us (3%)
    all_to_all x1, waiting for transfers between devices, shards(): lax.all_to_all(log_section, 'loc', split_axis=3, concat_axis=2, tiled=True)  180 us
    another operation x2, other arithmetic, survival(): hazard = jnp.cumsum(rates, axis=1)  45.5 us
    all_gather x1, waiting for transfers between devices, shards(): lax.all_gather(loc_factor, 'loc', axis=0, tiled=True)  38.4 us
    all_to_all x2, local copies, waits for them, and re-layouts, shards(): lax.all_to_all(log_section, 'loc', split_axis=3, concat_axis=2, tiled=True)  23.4 us
    dot_general x1, matrix products, shards(): jnp.einsum('ab,sbrl->sarl', age_factor, spread, preferred_element_type=jn...  21.3 us
    convert_element_type x1, local copies, waits for them, and re-layouts, shards(): log_section = (mean_rate[:, :, None, :] + mixed).astype(jnp.bfloat16)  12.3 us
    dot_general x1, matrix products, shards(): jnp.einsum('sarl,lg->sarg', population[:, :, None, :] * rates, onehot, pr...  12.1 us
  transfers between devices with their start and end apart: 3, of which 2 were waited for; matrix products, arithmetic and copies ran while one was open for 5% of the time, Pallas kernels for 0%

commit v1 on v0

--- a/solution.py
+++ b/solution.py
@@ -4,6 +4,18 @@
 from jax.sharding import PartitionSpec as P
 
 REGIONS = 64
+
+
+def in_blocks(x, dim, size):
+    lengths = x.shape
+    parts = x.reshape(*lengths[:dim], size, lengths[dim] // size, *lengths[dim + 1 :])
+    return jnp.moveaxis(parts, dim, 0)
+
+
+def joined_along(pieces, dim):
+    shape = list(pieces.shape[1:])
+    shape[dim] *= pieces.shape[0]
+    return jnp.moveaxis(pieces, 0, dim).reshape(shape)
 
 
 def survival(rates):
@@ -31,7 +43,14 @@
         "sarl,lg->sarg", population[:, :, None, :] * rates, onehot, precision=highest
     )
     region_section = survival(weighted / totals[:, :, None, :])
-    region_moved = lax.all_to_all(region_section, "loc", split_axis=2, concat_axis=1, tiled=True)
+    size, mine = (lax.axis_size("loc"), lax.axis_index("loc"))
+    blocks = in_blocks(region_section, 2, size)
+    outs = [blocks[mine]]
+    for hop in range(1, size):
+        sent = blocks[mine ^ hop]
+        outs.append(lax.ppermute(sent, "loc", [(i, i ^ hop) for i in range(size)]))
+    blocks = jnp.stack(outs)[mine ^ jnp.arange(size)]
+    region_moved = joined_along(blocks, 1)
     region_survival = jnp.transpose(region_moved, (0, 2, 1))
     turned = jnp.transpose(
         lax.all_to_all(log_section, "loc", split_axis=3, concat_axis=2, tiled=True), (0, 1, 3, 2)

time: 371 us -> 335 us (0.903); the launches traced: 370 us -> 330 us
  waiting for transfers between devices: 219 us -> 142 us
  starting transfers between devices: 11.7 us -> 50.7 us
    all_to_all x1, waiting for transfers between devices: 180 us -> 0.01 us  [shards(): lax.all_to_all(log_section, 'loc', split_axis=3, concat_axis=2, tiled=True)]
    ppermute x0 -> x15, waiting for transfers between devices: none -> 99.7 us  [shards(): outs.append(lax.ppermute(sent, 'loc', [(i, i ^ hop) for i in range(size)]))]
    ppermute x0 -> x15, starting transfers between devices: none -> 43.7 us  [shards(): outs.append(lax.ppermute(sent, 'loc', [(i, i ^ hop) for i in range(size)]))]
    all_to_all x1 -> x0, starting transfers between devices: 5.68 us -> none  [shards(): lax.all_to_all(region_section, 'loc', split_axis=2, concat_axis=1, tiled=...]
  transfers between devices with their start and end apart: 3 -> 17, of which waited for: 2 -> 11; matrix products, arithmetic and copies ran while one was open for 5% -> 17% of each run, Pallas kernels for 0% -> 0%
where the time goes in v1:
time: 335 us; the launch traced here: 330 us
  waiting for transfers between devices  142 us (42%)
  starting transfers between devices  50.7 us (15%)
  other arithmetic  47.3 us (14%)
  local copies, waits for them, and re-layouts  41 us (12%)
  matrix products  34.3 us (10%)
  between operations  14.2 us (4%)
    ppermute x15, waiting for transfers between devices, shards(): outs.append(lax.ppermute(sent, 'loc', [(i, i ^ hop) for i in range(size)]))  99.7 us
    another operation x2, other arithmetic, survival(): hazard = jnp.cumsum(rates, axis=1)  45.5 us
    ppermute x15, starting transfers between devices, shards(): outs.append(lax.ppermute(sent, 'loc', [(i, i ^ hop) for i in range(size)]))  43.7 us
    all_gather x1, waiting for transfers between devices, shards(): lax.all_gather(loc_factor, 'loc', axis=0, tiled=True)  41.9 us
    all_to_all x2, local copies, waits for them, and re-layouts, shards(): lax.all_to_all(log_section, 'loc', split_axis=3, concat_axis=2, tiled=True)  23.4 us
    dot_general x1, matrix products, shards(): jnp.einsum('ab,sbrl->sarl', age_factor, spread, preferred_element_type=jn...  21.3 us
    convert_element_type x1, local copies, waits for them, and re-layouts, shards(): log_section = (mean_rate[:, :, None, :] + mixed).astype(jnp.bfloat16)  12.4 us
    dot_general x1, matrix products, shards(): jnp.einsum('sarl,lg->sarg', population[:, :, None, :] * rates, onehot, pr...  12.1 us
  transfers between devices with their start and end apart: 17, of which 11 were waited for; matrix products, arithmetic and copies ran while one was open for 17% of the time, Pallas kernels for 0%

profile of v1, /device:TPU:11, one launch (start us, length us, event | category | flops | bytes accessed | tf_op | source)
XLA Modules:
  0.0 329.8 jit_solution(14680733655617433019)
XLA Ops:
  7.9 1.5 copy.53
  9.4 41.9 %all-gather.2.cloned.1.call-done = bf16[1024,1024]{1,0:T(8,128)(2,1)} async-done(((bf16[64,1024]{1,0:T(8,128)(2,1)}), bf16[1024,1024]{1,0:T(8,128)(2,1)}) %all-gather.2.cloned.1.call-update) | async-done | bytes 2097168 | tf_op jit(solution)/shard_map/all_gather | solution.py:34
  51.3 21.3 %fusion = bf16[2,111,16,1024]{3,1,2,0:T(8,128)(2,1)} fusion(f32[2,111,1024]{2,1,0:T(8,128)S(1)} %copy.53, bf16[2,111,16,1024]{3,2,1,0:T(8,128)(2,1)} %param.6, bf16[1024,1024]{1,0:T(8,128)(2,1)} %all-gather.2.cloned.1.call-done, bf16[111,111]{1,0:T(8,128)(2,1)S(1)} %copy-done), kind=kOutput, calls=%fused_computation.2 | convolution fusion | flops 8267464704 | bytes 17580098 | tf_op jit(solution)/shard_map/ab,sbrl->sarl/dot_general | solution.py:37
  72.6 12.4 %copy.55 = bf16[2,111,16,1024]{1,2,0,3:T(8,128)(2,1)} copy(bf16[2,111,16,1024]{3,1,2,0:T(8,128)(2,1)} %fusion) | data formatting | bytes 14548992 | tf_op jit(solution)/shard_map/convert_element_type | solution.py:38
  85.0 6.9 %all-to-all-start = ((bf16[2,111,16,1024]{1,2,0,3:T(8,128)(2,1)}), bf16[2,111,16,1024]{1,2,0,3:T(8,128)(2,1)}, u32[]{:S(2)}, u32[]{:S(2)}) async-start(bf16[2,111,16,1024]{1,2,0,3:T(8,128)(2,1)} %copy.55), calls=%async_computation | async-start | bytes 16777216 | tf_op jit(solution)/shard_map/all_to_all | solution.py:56
  92.0 1.2 copy.59
  94.0 12.1 %fusion.25 = f32[2,111,16,64]{1,3,2,0:T(8,128)S(1)} fusion(bf16[2,111,16,1024]{3,1,2,0:T(8,128)(2,1)} %fusion, f32[2,111,1024]{2,1,0:T(8,128)} %copy.59, f32[2,111,64]{1,2,0:T(8,128)S(1)} %convolution_bitcast_fusion, s32[1024]{0:T(1024)S(1)} %bitcast.118), kind=kOutput, calls=%fused_computation.19 | convolution fusion | flops 2800973824 | bytes 9154048 | tf_op jit(solution)/shard_map/sarl,lg->sarg/dot_general | solution.py:42
  106.2 0.9 copy.61
  107.0 36.4 %fusion.42 = f32[2,111,16,64]{3,2,1,0:T(8,128)S(1)} fusion(f32[2,111,16,64]{3,2,1,0:T(8,128)S(1)} %copy.61), kind=kOutput, calls=%fused_computation.70 | output fusion | flops 25006080 | bytes 1818624 | tf_op jit(solution)/shard_map/jit(cumsum)/reduce_window_sum | solution.py:22
  144.4 1.2 collective-permute-start.14
  145.7 1.2 collective-permute-start.13
  146.8 1.7 collective-permute-start.12
  149.1 2.2 collective-permute-done.1
  151.3 1.8 collective-permute-start.2
  153.1 1.3 collective-permute-done.2
  154.4 9.0 %collective-permute-start.3 = (f32[2,16,4]{1,2,0:T(4,128)S(1)}, f32[2,16,4]{1,2,0:T(4,128)S(1)}, u32[]{:S(2)}, u32[]{:S(2)}) collective-permute-start(f32[2,16,4]{1,2,0:T(4,128)S(1)} %get-tuple-element.25), channel_id=1, source_target_pairs={{0,8},{2,10},{4,12},{6,14},{8,0},{10,2},{12,4},{14,6},{16,24},{18,... | collective-permute-start | bytes 1544 | tf_op jit(solution)/shard_map/ppermute | solution.py:51
  163.4 66.4 %collective-permute-done.3 = f32[2,16,4]{1,2,0:T(4,128)S(1)} collective-permute-done((f32[2,16,4]{1,2,0:T(4,128)S(1)}, f32[2,16,4]{1,2,0:T(4,128)S(1)}, u32[]{:S(2)}, u32[]{:S(2)}) %collective-permute-start.3) | collective-permute-done | bytes 544 | tf_op jit(solution)/shard_map/ppermute | solution.py:51
  229.8 3.0 collective-permute-done.4
  232.8 3.3 %collective-permute-done.5 = f32[2,16,4]{1,2,0:T(4,128)S(1)} collective-permute-done((f32[2,16,4]{1,2,0:T(4,128)S(1)}, f32[2,16,4]{1,2,0:T(4,128)S(1)}, u32[]{:S(2)}, u32[]{:S(2)}) %collective-permute-start.5) | collective-permute-done | bytes 544 | tf_op jit(solution)/shard_map/ppermute | solution.py:51
  236.2 18.4 %collective-permute-start.6 = (f32[2,16,4]{1,2,0:T(4,128)S(1)}, f32[2,16,4]{1,2,0:T(4,128)S(1)}, u32[]{:S(2)}, u32[]{:S(2)}) collective-permute-start(f32[2,16,4]{1,2,0:T(4,128)S(1)} %get-tuple-element.22), channel_id=1, source_target_pairs={{0,14},{2,12},{4,10},{6,8},{8,6},{10,4},{12,2},{14,0},{16,30},{18,... | collective-permute-start | bytes 1544 | tf_op jit(solution)/shard_map/ppermute | solution.py:51
  254.6 1.3 collective-permute-done.6
  255.9 17.0 %collective-permute-done.7 = f32[2,16,4]{1,2,0:T(4,128)S(1)} collective-permute-done((f32[2,16,4]{1,2,0:T(4,128)S(1)}, f32[2,16,4]{1,2,0:T(4,128)S(1)}, u32[]{:S(2)}, u32[]{:S(2)}) %collective-permute-start.7) | collective-permute-done | bytes 544 | tf_op jit(solution)/shard_map/ppermute | solution.py:51
  272.9 3.9 %collective-permute-start.8 = (f32[2,16,4]{1,2,0:T(4,128)S(1)}, f32[2,16,4]{1,2,0:T(4,128)S(1)}, u32[]{:S(2)}, u32[]{:S(2)}) collective-permute-start(f32[2,16,4]{1,2,0:T(4,128)S(1)} %get-tuple-element.20), channel_id=1, source_target_pairs={{0,18},{2,16},{4,22},{6,20},{8,26},{10,24},{12,30},{14,28},{16,2},... | collective-permute-start | bytes 1544 | tf_op jit(solution)/shard_map/ppermute | solution.py:51
  276.7 1.3 collective-permute-done.8
  278.0 1.7 collective-permute-start.9
  279.7 2.6 collective-permute-done.9
  282.3 3.9 %collective-permute-start.10 = (f32[2,16,4]{1,2,0:T(4,128)S(1)}, f32[2,16,4]{1,2,0:T(4,128)S(1)}, u32[]{:S(2)}, u32[]{:S(2)}) collective-permute-start(f32[2,16,4]{1,2,0:T(4,128)S(1)} %get-tuple-element.18), channel_id=1, source_target_pairs={{0,22},{2,20},{4,18},{6,16},{8,30},{10,28},{12,26},{14,24},{16,6},... | collective-permute-start | bytes 1544 | tf_op jit(solution)/shard_map/ppermute | solution.py:51
  286.2 1.3 collective-permute-done.10
  288.9 9.9 %copy.57 = bf16[2,111,16,16,64]{1,4,3,2,0:T(8,128)(2,1)} copy(bf16[2,111,16,16,64]{1,3,0,4,2:T(8,128)(2,1)} %bitcast.7) | data formatting | bytes 14548992 | tf_op jit(solution)/shard_map/all_to_all | solution.py:56
  298.8 13.5 %copy.58 = bf16[2,111,256,64]{2,3,1,0:T(8,128)(2,1)} copy(bf16[2,111,256,64]{1,3,2,0:T(8,128)(2,1)} %bitcast.110) | data formatting | bytes 14548992 | tf_op jit(solution)/shard_map/all_to_all | solution.py:56
  312.3 9.1 %fusion.41 = (f32[2,64,256]{2,1,0:T(8,128)S(1)}, f32[2,111,64,256]{3,2,1,0:T(8,128)}) fusion(bf16[2,111,64,256]{3,2,1,0:T(8,128)(2,1)} %bitcast.111), kind=kOutput, calls=%fused_computation.69 | output fusion | flops 410976256 | bytes 21954560 | tf_op jit(solution)/shard_map/jit(cumsum)/reduce_window_sum | solution.py:22
  321.4 1.6 fusion.34
  (51 shorter events, 4.5 us)
Async XLA Ops:
  7.2 44.1 %copy-start = (bf16[111,111]{1,0:T(8,128)(2,1)S(1)}, bf16[111,111]{1,0:T(8,128)(2,1)}, u32[]{:S(2)}) copy-start(bf16[111,111]{1,0:T(8,128)(2,1)} %param.8) | copy-start | bytes 73930
  7.2 44.1 %all-gather.2.cloned.1.call-start = ((), (), s32[]{:S(2)}) async-start(), calls=%async_computation.1 | async-start | bytes 2228224 | tf_op jit(solution)/shard_map/all_gather | solution.py:34
  85.0 6.9 %copy-start.2 = (f32[2,111,1024]{2,0,1:T(2,128)S(1)}, f32[2,111,1024]{2,0,1:T(2,128)}, u32[]{:S(2)}) copy-start(f32[2,111,1024]{2,0,1:T(2,128)} %param.10) | copy-start | bytes 2727940
  85.0 8.2 %copy-start.3 = (s32[1024,1]{0,1:T(1,128)S(1)}, s32[1024,1]{0,1:T(1,128)}, u32[]{:S(2)}) copy-start(s32[1024,1]{0,1:T(1,128)} %param.11) | copy-start | bytes 12292
  85.0 203.9 %all-to-all-start = ((bf16[2,111,16,1024]{1,2,0,3:T(8,128)(2,1)}), bf16[2,111,16,1024]{1,2,0,3:T(8,128)(2,1)}, u32[]{:S(2)}, u32[]{:S(2)}) async-start(bf16[2,111,16,1024]{1,2,0,3:T(8,128)(2,1)} %copy.55), calls=%async_computation | async-start | bytes 16777216 | tf_op jit(solution)/shard_map/all_to_all | solution.py:56
  144.0 4.8 %collective-permute-start = (f32[2,16,4]{1,2,0:T(4,128)S(1)}, f32[2,16,4]{1,2,0:T(4,128)S(1)}, u32[]{:S(2)}, u32[]{:S(2)}) collective-permute-start(f32[2,16,4]{1,2,0:T(4,128)S(1)} %get-tuple-element.28), channel_id=1, source_target_pairs={{0,2},{2,0},{4,6},{6,4},{8,10},{10,8},{12,14},{14,12},{16,18},{18,... | collective-permute-start | bytes 1544 | tf_op jit(solution)/shard_map/ppermute | solution.py:51
  144.4 143.2 %collective-permute-start.14 = (f32[2,16,4]{1,2,0:T(4,128)S(1)}, f32[2,16,4]{1,2,0:T(4,128)S(1)}, u32[]{:S(2)}, u32[]{:S(2)}) collective-permute-start(f32[2,16,4]{1,2,0:T(4,128)S(1)} %get-tuple-element.14), channel_id=1, source_target_pairs={{0,30},{2,28},{4,26},{6,24},{8,22},{10,20},{12,18},{14,16},{16,14}... | collective-permute-start | bytes 1544 | tf_op jit(solution)/shard_map/ppermute | solution.py:51
  145.7 141.9 %collective-permute-start.13 = (f32[2,16,4]{1,2,0:T(4,128)S(1)}, f32[2,16,4]{1,2,0:T(4,128)S(1)}, u32[]{:S(2)}, u32[]{:S(2)}) collective-permute-start(f32[2,16,4]{1,2,0:T(4,128)S(1)} %get-tuple-element.15), channel_id=1, source_target_pairs={{0,28},{2,30},{4,24},{6,26},{8,20},{10,22},{12,16},{14,18},{16,12}... | collective-permute-start | bytes 1544 | tf_op jit(solution)/shard_map/ppermute | solution.py:51
  146.8 140.7 %collective-permute-start.12 = (f32[2,16,4]{1,2,0:T(4,128)S(1)}, f32[2,16,4]{1,2,0:T(4,128)S(1)}, u32[]{:S(2)}, u32[]{:S(2)}) collective-permute-start(f32[2,16,4]{1,2,0:T(4,128)S(1)} %get-tuple-element.16), channel_id=1, source_target_pairs={{0,26},{2,24},{4,30},{6,28},{8,18},{10,16},{12,22},{14,20},{16,10}... | collective-permute-start | bytes 1544 | tf_op jit(solution)/shard_map/ppermute | solution.py:51
  148.5 139.0 %collective-permute-start.11 = (f32[2,16,4]{1,2,0:T(4,128)S(1)}, f32[2,16,4]{1,2,0:T(4,128)S(1)}, u32[]{:S(2)}, u32[]{:S(2)}) collective-permute-start(f32[2,16,4]{1,2,0:T(4,128)S(1)} %get-tuple-element.17), channel_id=1, source_target_pairs={{0,24},{2,26},{4,28},{6,30},{8,16},{10,18},{12,20},{14,22},{16,8},... | collective-permute-start | bytes 1544 | tf_op jit(solution)/shard_map/ppermute | solution.py:51
  148.8 2.5 collective-permute-start.1
  151.3 3.1 collective-permute-start.2
  154.4 75.4 %collective-permute-start.3 = (f32[2,16,4]{1,2,0:T(4,128)S(1)}, f32[2,16,4]{1,2,0:T(4,128)S(1)}, u32[]{:S(2)}, u32[]{:S(2)}) collective-permute-start(f32[2,16,4]{1,2,0:T(4,128)S(1)} %get-tuple-element.25), channel_id=1, source_target_pairs={{0,8},{2,10},{4,12},{6,14},{8,0},{10,2},{12,4},{14,6},{16,24},{18,... | collective-permute-start | bytes 1544 | tf_op jit(solution)/shard_map/ppermute | solution.py:51
  229.8 3.0 collective-permute-start.4
  232.8 3.4 %collective-permute-start.5 = (f32[2,16,4]{1,2,0:T(4,128)S(1)}, f32[2,16,4]{1,2,0:T(4,128)S(1)}, u32[]{:S(2)}, u32[]{:S(2)}) collective-permute-start(f32[2,16,4]{1,2,0:T(4,128)S(1)} %get-tuple-element.23), channel_id=1, source_target_pairs={{0,12},{2,14},{4,8},{6,10},{8,4},{10,6},{12,0},{14,2},{16,28},{18,... | collective-permute-start | bytes 1544 | tf_op jit(solution)/shard_map/ppermute | solution.py:51
  236.2 19.7 %collective-permute-start.6 = (f32[2,16,4]{1,2,0:T(4,128)S(1)}, f32[2,16,4]{1,2,0:T(4,128)S(1)}, u32[]{:S(2)}, u32[]{:S(2)}) collective-permute-start(f32[2,16,4]{1,2,0:T(4,128)S(1)} %get-tuple-element.22), channel_id=1, source_target_pairs={{0,14},{2,12},{4,10},{6,8},{8,6},{10,4},{12,2},{14,0},{16,30},{18,... | collective-permute-start | bytes 1544 | tf_op jit(solution)/shard_map/ppermute | solution.py:51
  255.9 17.0 %collective-permute-start.7 = (f32[2,16,4]{1,2,0:T(4,128)S(1)}, f32[2,16,4]{1,2,0:T(4,128)S(1)}, u32[]{:S(2)}, u32[]{:S(2)}) collective-permute-start(f32[2,16,4]{1,2,0:T(4,128)S(1)} %get-tuple-element.21), channel_id=1, source_target_pairs={{0,16},{2,18},{4,20},{6,22},{8,24},{10,26},{12,28},{14,30},{16,0},... | collective-permute-start | bytes 1544 | tf_op jit(solution)/shard_map/ppermute | solution.py:51
  272.9 5.1 %collective-permute-start.8 = (f32[2,16,4]{1,2,0:T(4,128)S(1)}, f32[2,16,4]{1,2,0:T(4,128)S(1)}, u32[]{:S(2)}, u32[]{:S(2)}) collective-permute-start(f32[2,16,4]{1,2,0:T(4,128)S(1)} %get-tuple-element.20), channel_id=1, source_target_pairs={{0,18},{2,16},{4,22},{6,20},{8,26},{10,24},{12,30},{14,28},{16,2},... | collective-permute-start | bytes 1544 | tf_op jit(solution)/shard_map/ppermute | solution.py:51
  278.0 4.3 %collective-permute-start.9 = (f32[2,16,4]{1,2,0:T(4,128)S(1)}, f32[2,16,4]{1,2,0:T(4,128)S(1)}, u32[]{:S(2)}, u32[]{:S(2)}) collective-permute-start(f32[2,16,4]{1,2,0:T(4,128)S(1)} %get-tuple-element.19), channel_id=1, source_target_pairs={{0,20},{2,22},{4,16},{6,18},{8,28},{10,30},{12,24},{14,26},{16,4},... | collective-permute-start | bytes 1544 | tf_op jit(solution)/shard_map/ppermute | solution.py:51
  282.3 5.2 %collective-permute-start.10 = (f32[2,16,4]{1,2,0:T(4,128)S(1)}, f32[2,16,4]{1,2,0:T(4,128)S(1)}, u32[]{:S(2)}, u32[]{:S(2)}) collective-permute-start(f32[2,16,4]{1,2,0:T(4,128)S(1)} %get-tuple-element.18), channel_id=1, source_target_pairs={{0,22},{2,20},{4,18},{6,16},{8,30},{10,28},{12,26},{14,24},{16,6},... | collective-permute-start | bytes 1544 | tf_op jit(solution)/shard_map/ppermute | solution.py:51
  312.3 10.7 %copy-start.1 = (bf16[111,111]{1,0:T(8,128)(2,1)S(1)}, bf16[111,111]{1,0:T(8,128)(2,1)}, u32[]{:S(2)}) copy-start(bf16[111,111]{1,0:T(8,128)(2,1)} %param.8) | copy-start | bytes 73930
Sparse Core Ops, SparseCore 0:
  10.2 41.0 all-gather.1
